TPU v7x, 512 devices: a whole 4x4x16 slice. The times are simulated.
512 devices in a mesh: lon: 64 (over x_hi, z, core), tp: 8 (over y, x_lo).
Axes of the slice: x: 4 (x_hi: 2, x_lo: 2; x = x_hi * 2 + x_lo), y: 4, z: 16, core: 2. Of those that a mesh axis runs over, the one named last changes fastest.
Arguments:
- image_tokens: bfloat16 [16384, 3072], P('lon', 'tp'), may hold values from -6 to 6
- style_tokens: bfloat16 [2048, 3072], P('lon', 'tp'), may hold values from -6 to 6
- qkv_weight: bfloat16 [3, 3072, 2048], P(None, 'lon', 'tp'), may hold values from -0.109375 to 0.109375
- out_weight: bfloat16 [2048, 3072], P('tp', 'lon'), may hold values from -0.125 to 0.125
- query_gain: float32 [128], replicated, may hold values from 0.6 to 9, as said below
- key_gain: float32 [128], replicated, may hold values from 0.6 to 9, as said below
- attend_flags: int32 [64, 1], P('lon'), may hold values from 0 to 1
Outputs:
- mixed: bfloat16 [16384, 3072], P('lon', 'tp')
Inputs may be any that keep to these rules, and one draw needn't show every extreme that they name: `query_gain`: positive gains. `key_gain`: positive gains.
All inputs are finite; a program needn't handle non-finite values.
Results may differ from a plain program's by a relative error of at most 0.015.
The roundings to bfloat16 on the way count: a program that leaves them out, or rounds other values in their place, can miss the bound.
Values may be sent and summed in bfloat16 or wider, within the bound.
No kernel may reach another device: no remote copies, remote signals or barrier semaphores. Data moves between devices by JAX's collectives and lax.ppermute only.
A program may use at most 64 MiB of HBM per device.

v0:
```python
import functools
import math

import jax
import jax.numpy as jnp
from jax import lax
from jax.experimental import pallas as pl
from jax.experimental.pallas import tpu as pltpu
from jax.sharding import Mesh, PartitionSpec as P


HEAD = 128
AXES = ("x_hi", "z_hi", "z_lo", "core", "y", "x_lo")
Z = ("z_hi", "z_lo")
LON = ("x_hi",) + Z + ("core",)
TP = ("y", "x_lo")
F32 = jnp.float32
BF16 = jnp.bfloat16


def spread(block, axes):
    count = lax.axis_size(axes)
    return lax.all_to_all(
        jnp.broadcast_to(block[None], (count,) + block.shape), axes, 0, 0, tiled=True
    )


def unit(values, gain):
    return values * lax.rsqrt(jnp.mean(values * values, axis=-1, keepdims=True) + 1e-06) * gain


def pack_kernel(w_ref, o_ref, out_ref):
    copies = out_ref.shape[0] * HEAD // w_ref.shape[2]
    for c in range(w_ref.shape[2] // HEAD):
        lanes = pl.ds(c * HEAD, HEAD)
        row = jnp.concatenate(
            [w_ref[1, :, lanes], w_ref[2, :, lanes], w_ref[0, :, lanes], o_ref[:, lanes]], axis=1
        )
        for r in range(copies):
            out_ref[r * (w_ref.shape[2] // HEAD) + c] = row


def pack(w, o, copies):
    heads = w.shape[2] // HEAD
    return pl.pallas_call(
        pack_kernel,
        out_shape=jax.ShapeDtypeStruct((copies * heads, w.shape[1], 4 * HEAD), BF16),
        name="pack",
    )(w, o)


def project_kernel(
    me_ref,
    x_ref,
    y_ref,
    sx_ref,
    sy_ref,
    w_ref,
    qg_ref,
    kg_ref,
    forward_ref,
    backward_ref,
    low_ref,
    high_ref,
    q_ref,
    acc,
    qacc,
    tokens,
    weights,
    arrived,
):
    steps, total, wide = tokens.shape
    _, count, width = x_ref.shape
    groups, _, rows, _ = sx_ref.shape
    pieces = wide // width
    far = total - 2 * count

    def fetches(step):
        sources = [(r, (), count) for r in (x_ref, y_ref)]
        sources += [(r, (g,), rows) for r in (sx_ref, sy_ref) for g in range(groups)]
        found = [(w_ref.at[pl.ds(step * wide, wide), pl.ds(0, 3 * HEAD)], weights.at[step])]
        for j in range(pieces):
            at = 0
            for r, i, n in sources:
                lines, lanes = pl.ds(at, n), pl.ds(j * width, width)
                found.append((r.at[i + (step * pieces + j,)], tokens.at[step, lines, lanes]))
                at += n
        return [
            pltpu.make_async_copy(a, b, arrived.at[step, n]) for n, (a, b) in enumerate(found)
        ]

    for step in range(steps):
        for copy in fetches(step):
            copy.start()
    acc[...] = jnp.zeros_like(acc)
    qacc[...] = jnp.zeros_like(qacc)

    @pl.loop(0, steps)
    def _(step):
        for copy in fetches(step):
            copy.wait()
        w = weights[step]
        acc[...] += jnp.dot(tokens[step], w[:, : 2 * HEAD], preferred_element_type=F32)
        qacc[...] += jnp.dot(
            tokens[step, : 2 * count], w[:, 2 * HEAD :], preferred_element_type=F32
        )

    kg, qg = kg_ref[...], qg_ref[...]
    for half, part_ref in enumerate((low_ref, high_ref)):
        lines = pl.ds(half * far // 2, far // 2)
        source = pl.ds(2 * count + half * far // 2, far // 2)
        k = unit(acc[source, :HEAD], kg).astype(BF16)
        v = acc[source, HEAD:].astype(BF16)
        for out_ref in (forward_ref, backward_ref):
            out_ref[lines, :HEAD] = k
            out_ref[lines, HEAD:] = v
        part_ref[:, :HEAD] = k
        part_ref[:, HEAD:] = v
    me = me_ref[0]
    lines = pl.ds(far, count)
    for slab, out_ref in enumerate((backward_ref, forward_ref)):
        mine = pl.ds(pl.multiple_of((slab ^ me) * count, count), count)
        out_ref[lines, :HEAD] = unit(acc[mine, :HEAD], kg).astype(BF16)
        out_ref[lines, HEAD:] = acc[mine, HEAD:].astype(BF16)
        q_ref[slab] = unit(qacc[mine], qg).astype(BF16)


def project(me, slabs, styles, w, query_gain, key_gain):
    parts, count, width = slabs[0].shape
    groups, _, rows, _ = styles[0].shape
    pieces = 2
    steps = parts // pieces
    far = 2 * groups * rows
    total = 2 * count + far
    shapes = [(far + count, 2 * HEAD)] * 2 + [(far // 2, 2 * HEAD)] * 2 + [(2, count, HEAD)]
    vmem = pl.BlockSpec(memory_space=pltpu.VMEM)
    hbm = pl.BlockSpec(memory_space=pltpu.HBM)
    return pl.pallas_call(
        project_kernel,
        in_specs=[pl.BlockSpec(memory_space=pltpu.SMEM)] + [hbm] * 5 + [vmem] * 2,
        out_specs=[vmem] * len(shapes),
        out_shape=[jax.ShapeDtypeStruct(shape, BF16) for shape in shapes],
        scratch_shapes=[
            pltpu.VMEM((total, 2 * HEAD), F32),
            pltpu.VMEM((2 * count, HEAD), F32),
            pltpu.VMEM((steps, total, pieces * width), BF16),
            pltpu.VMEM((steps, pieces * width, 3 * HEAD), BF16),
            pltpu.SemaphoreType.DMA((steps, 1 + pieces * (2 + 2 * groups))),
        ],
        compiler_params=pltpu.CompilerParams(vmem_limit_bytes=60 << 20),
        name="project",
    )(me, *slabs, *styles, w, query_gain, key_gain)


NT = (((1,), (1,)), ((), ()))


def attend_kernel(
    turn,
    me_ref,
    flag_ref,
    q_ref,
    forward_ref,
    backward_ref,
    before_ref,
    after_ref,
    low_ref,
    high_ref,
    o_ref,
    near,
):
    slab = me_ref[0] ^ turn
    count = q_ref.shape[1]
    style = forward_ref.shape[0] - count
    lines = pl.ds(style, count)
    near[pl.ds(0, count)] = backward_ref[lines]
    near[pl.ds(count, count)] = forward_ref[lines]

    @pl.when(slab == 0)
    def _():
        near[pl.ds(2 * count, count)] = before_ref[lines]

    @pl.when(slab == 1)
    def _():
        near[pl.ds(2 * count, count)] = after_ref[lines]

    scale = 1.0 / math.sqrt(HEAD)
    q = q_ref[slab]
    lines = pl.ds(0, style)
    refs = [near, *(r.at[lines] for r in (forward_ref, before_ref, after_ref)), low_ref, high_ref]
    scores = []
    for n, ref in enumerate(refs):
        part = lax.dot_general(q, ref[:, :HEAD], NT, preferred_element_type=F32) * scale
        scores.append(jnp.where(flag_ref[0, 0] > 0, part, -1e30) if n else part)
    peak = functools.reduce(jnp.maximum, [jnp.max(s, axis=-1, keepdims=True) for s in scores])
    expo = [jnp.exp(s - peak) for s in scores]
    share = 1.0 / sum(jnp.sum(e, axis=-1, keepdims=True) for e in expo)
    o_ref[...] = sum(
        jnp.dot((e * share).astype(BF16), ref[:, HEAD:], preferred_element_type=F32)
        for e, ref in zip(expo, refs)
    ).astype(BF16)


def attend(turn, me, flag, query, *keys):
    count = query.shape[1]
    scalar = pl.BlockSpec(memory_space=pltpu.SMEM)
    vmem = pl.BlockSpec(memory_space=pltpu.VMEM)
    return pl.pallas_call(
        functools.partial(attend_kernel, turn),
        in_specs=[scalar] * 2 + [vmem] * (1 + len(keys)),
        out_specs=vmem,
        out_shape=jax.ShapeDtypeStruct((count, HEAD), BF16),
        scratch_shapes=[pltpu.VMEM((3 * count, 2 * HEAD), BF16)],
        compiler_params=pltpu.CompilerParams(vmem_limit_bytes=24 << 20),
        cost_estimate=pl.CostEstimate(
            flops=11 * 256 * 256 * 4 * HEAD, bytes_accessed=2 << 20, transcendentals=11 << 16
        ),
    )(me, flag, query, *keys)


def mix_kernel(ax_ref, ay_ref, wx_ref, wy_ref, o_ref):
    parts, _, width = o_ref.shape
    a = jnp.concatenate([ax_ref[...], ay_ref[...]], axis=1)
    for i in range(parts):
        lines = pl.ds(i * width, width)
        w = jnp.concatenate([wx_ref[lines], wy_ref[lines]], axis=1)
        o_ref[i] = lax.dot_general(a, w, NT, preferred_element_type=F32).astype(BF16)


def mix(attended, panels, parts):
    count = attended[0].shape[0]
    width = panels[0].shape[0] // parts
    return pl.pallas_call(
        mix_kernel,
        out_shape=jax.ShapeDtypeStruct((parts, count, width), BF16),
        compiler_params=pltpu.CompilerParams(vmem_limit_bytes=12 << 20),
        name="mix",
    )(*attended, *panels)


def local(image_tokens, style_tokens, qkv_weight, out_weight, query_gain, key_gain, attend_flags):
    parts = lax.axis_size(TP)
    cores = lax.axis_size("core")
    halves = lax.axis_size("x_hi")
    rows = lax.axis_size(Z)
    depth = qkv_weight.shape[1]

    def swap(block):
        return lax.ppermute(block, "core", [(0, 1), (1, 0)])

    me = lax.axis_index("core").reshape(1)
    mine = pack(qkv_weight, out_weight.T, halves)
    plane = lax.all_to_all(mine, ("x_hi", "core"), 0, 0, tiled=True)
    plane = plane.reshape(halves, cores * depth, 4 * HEAD)
    panel = lax.all_gather(plane, Z, axis=1, tiled=True).reshape(-1, 4 * HEAD)

    image_tokens, style_tokens, attend_flags, _ = lax.optimization_barrier(
        (image_tokens, style_tokens, attend_flags, plane)
    )

    def shift(block, axes, count, by):
        return lax.ppermute(block, axes, [(i, (i + by) % count) for i in range(count)])

    step = rows // 4
    style = [style_tokens]
    style += [shift(style_tokens, Z, rows, i * step) for i in (1, 2, 3)]
    style = jnp.concatenate(style, axis=0)
    own = spread(image_tokens, TP)
    slabs = (own, swap(own))
    style = spread(style, ("x_hi",) + TP)
    style = style.reshape((halves, parts) + style.shape[1:])
    styles = (style, swap(style))
    flags = (attend_flags, swap(attend_flags))
    slabs, styles, flags = lax.optimization_barrier((slabs, styles, flags))

    forward, backward, low, high, query = project(
        me, slabs, styles, panel, query_gain.reshape(1, HEAD), key_gain.reshape(1, HEAD)
    )
    chips = halves * rows
    before = shift(forward, ("x_hi",) + Z, chips, 1)
    after = shift(backward, ("x_hi",) + Z, chips, -1)
    low = shift(low, Z, rows, 2)
    high = shift(high, Z, rows, -2)
    panel, query = lax.optimization_barrier((panel, query))
    out_own = panel[:, 3 * HEAD :]
    out_other = swap(out_own)

    keys = (forward, backward, before, after, low, high)
    theirs = swap(attend(1, me, flags[1], query, *keys))
    mine = attend(0, me, flags[0], query, *keys)
    shares = mix((mine, theirs), (out_own, out_other), parts)
    shares = lax.all_to_all(shares, TP, 0, 0, tiled=True)
    return jnp.sum(shares.astype(F32), axis=0).astype(BF16)


def solution(mesh):
    fine = Mesh(mesh.devices.reshape(2, 4, 4, 2, 4, 2), AXES)
    in_specs = (
        P(LON, TP),
        P(LON, TP),
        P(None, LON, TP),
        P(TP, LON),
        P(),
        P(),
        P(LON, None),
    )
    return jax.shard_map(
        local, mesh=fine, in_specs=in_specs, out_specs=P(LON, TP), check_vma=False
    )
```

profile of v0, /device:TPU:1, one launch (start us, length us, event | category | flops | bytes accessed | tf_op | source)
XLA Modules:
  0.0 176.5 jit_solution(14295460600703613131)
XLA Ops:
  6.5 0.0 all-gather.2.cloned.1.call-start
  6.5 1.6 pack.1
  8.1 17.0 %all_to_all.20 = bf16[4,48,512]{2,1,0:T(8,128)(2,1)} all-to-all(bf16[4,48,512]{2,1,0:T(8,128)(2,1)} %pack.1), channel_id=1, replica_groups=mesh['x_hi'=2,'z_hi'=4,'z_lo'=4,'core'=2,'y'=4,'x_lo'=2] {'x_hi','core'}, dimensions={0} | all-to-all | bytes 393216 | tf_op jit(solution)/shard_map/all_to_all | solution.py:253
  25.1 0.0 all-gather.2.cloned.1.call-update
  25.1 2.2 %broadcast_in_dim.4 = bf16[8,256,384]{2,1,0:T(8,128)(2,1)} broadcast(bf16[256,384]{1,0:T(8,128)(2,1)} %param.7), dimensions={1,2} | broadcast | bytes 1769472 | tf_op jit(solution)/shard_map/broadcast_in_dim | solution.py:24
  27.3 3.7 %all-to-all-start.1 = ((bf16[8,256,384]{2,1,0:T(8,128)(2,1)}), bf16[8,256,384]{2,1,0:T(8,128)(2,1)S(1)}, u32[]{:S(2)}, u32[]{:S(2)}) async-start(bf16[8,256,384]{2,1,0:T(8,128)(2,1)} %broadcast_in_dim.4), calls=%async_computation.1 | async-start | bytes 3145728 | tf_op jit(solution)/shard_map/all_to_all | solution.py:23
  31.1 0.0 copy-done.5
  31.1 5.0 %collective-permute-start.1 = (bf16[32,384]{1,0:T(8,128)(2,1)S(1)}, bf16[32,384]{1,0:T(8,128)(2,1)S(1)}, u32[]{:S(2)}, u32[]{:S(2)}) collective-permute-start(bf16[32,384]{1,0:T(8,128)(2,1)S(1)} %copy-done.5), channel_id=1, source_target_pairs={{0,64},{16,80},{32,96},{48,112},{64,128},{80,144},{96,160},{112,17... | collective-permute-start | bytes 73736 | tf_op jit(solution)/shard_map/ppermute | solution.py:262
  36.1 10.6 %collective-permute-start.2 = (bf16[32,384]{1,0:T(8,128)(2,1)S(1)}, bf16[32,384]{1,0:T(8,128)(2,1)S(1)}, u32[]{:S(2)}, u32[]{:S(2)}) collective-permute-start(bf16[32,384]{1,0:T(8,128)(2,1)S(1)} %copy-done.5), channel_id=1, source_target_pairs={{0,128},{16,144},{32,160},{48,176},{64,192},{80,208},{96,224},{112... | collective-permute-start | bytes 73736 | tf_op jit(solution)/shard_map/ppermute | solution.py:262
  46.7 5.2 %collective-permute-start.3 = (bf16[32,384]{1,0:T(8,128)(2,1)S(1)}, bf16[32,384]{1,0:T(8,128)(2,1)S(1)}, u32[]{:S(2)}, u32[]{:S(2)}) collective-permute-start(bf16[32,384]{1,0:T(8,128)(2,1)S(1)} %copy-done.5), channel_id=1, source_target_pairs={{0,192},{16,208},{32,224},{48,240},{64,0},{80,16},{96,32},{112,48}... | collective-permute-start | bytes 73736 | tf_op jit(solution)/shard_map/ppermute | solution.py:262
  51.9 0.0 collective-permute-done.1
  51.9 0.0 collective-permute-done.2
  51.9 4.3 %collective-permute-done.3 = bf16[32,384]{1,0:T(8,128)(2,1)S(1)} collective-permute-done((bf16[32,384]{1,0:T(8,128)(2,1)S(1)}, bf16[32,384]{1,0:T(8,128)(2,1)S(1)}, u32[]{:S(2)}, u32[]{:S(2)}) %collective-permute-start.3) | collective-permute-done | bytes 24608 | tf_op jit(solution)/shard_map/ppermute | solution.py:262
  56.2 0.0 all-to-all-done.1.x_ref
  56.2 1.5 broadcast_in_dim.5
  57.7 5.0 %all-to-all-start.2 = ((bf16[16,128,384]{2,1,0:T(8,128)(2,1)}), bf16[16,128,384]{2,1,0:T(8,128)(2,1)S(1)}, u32[]{:S(2)}, u32[]{:S(2)}) async-start(bf16[16,128,384]{2,1,0:T(8,128)(2,1)} %broadcast_in_dim.5), calls=%async_computation.2 | async-start | bytes 3145728 | tf_op jit(solution)/shard_map/all_to_all | solution.py:23
  62.8 0.0 copy-done.3
  62.8 5.2 %collective-permute-start = (bf16[8,256,384]{2,1,0:T(8,128)(2,1)S(1)}, bf16[8,256,384]{2,1,0:T(8,128)(2,1)}, u32[]{:S(2)}, u32[]{:S(2)}) collective-permute-start(bf16[8,256,384]{2,1,0:T(8,128)(2,1)S(1)} %all-to-all-done.1.x_ref), channel_id=1, source_target_pairs={{0,8},{8,0},{1,9},{9,1},{2,10},{10,2},{3,11},{11,3},{4,12},{12,4},... | collective-permute-start | bytes 4718600 | tf_op jit(solution)/shard_map/ppermute | solution.py:249
  67.9 14.4 %all-to-all-done.2 = bf16[16,128,384]{2,1,0:T(8,128)(2,1)S(1)} async-done(((bf16[16,128,384]{2,1,0:T(8,128)(2,1)}), bf16[16,128,384]{2,1,0:T(8,128)(2,1)S(1)}, u32[]{:S(2)}, u32[]{:S(2)}) %all-to-all-start.2) | async-done | bytes 1572896 | tf_op jit(solution)/shard_map/all_to_all | solution.py:23
  82.4 6.2 %collective-permute-start.4 = (bf16[2,8,128,384]{3,2,1,0:T(8,128)(2,1)S(1)}, bf16[2,8,128,384]{3,2,1,0:T(8,128)(2,1)}, u32[]{:S(2)}, u32[]{:S(2)}) collective-permute-start(bf16[2,8,128,384]{3,2,1,0:T(8,128)(2,1)S(1)} %bitcast.7), channel_id=1, source_target_pairs={{0,8},{8,0},{1,9},{9,1},{2,10},{10,2},{3,11},{11,3},{4,12},{12,4},... | collective-permute-start | bytes 4718600 | tf_op jit(solution)/shard_map/ppermute | solution.py:249
  88.6 1.9 %collective-permute-start.5 = (s32[1,1]{1,0:T(1,128)}, s32[1,1]{1,0:T(1,128)}, u32[]{:S(2)}, u32[]{:S(2)}) collective-permute-start(s32[1,1]{1,0:T(1,128)} %param.13), channel_id=1, source_target_pairs={{0,8},{8,0},{1,9},{9,1},{2,10},{10,2},{3,11},{11,3},{4,12},{12,4},... | collective-permute-start | bytes 20 | tf_op jit(solution)/shard_map/ppermute | solution.py:249
  90.6 1.2 collective-permute-done.5.flag_ref
  91.8 0.0 collective-permute-done.y_ref
  91.8 0.0 collective-permute-done.4.sy_ref
  91.8 1.0 all-gather.2.cloned.1.call-done
  92.8 0.0 copy-done.4
  92.8 7.1 %project.1 = (bf16[768,256]{1,0:T(8,128)(2,1)}, bf16[768,256]{1,0:T(8,128)(2,1)}, bf16[256,256]{1,0:T(8,128)(2,1)}, bf16[256,256]{1,0:T(8,128)(2,1)}, bf16[2,256,128]{2,1,0:T(8,128)(2,1)}) custom-call(s32[1]{0:T(128)} %bitcast.me_ref, bf16[8,256,384]{2,1,0:T(8,128)(2,1)} %copy-done.3, bf16[8,256,384]{2,1,0:T(8,128)(2,1)} %collective-permute-done.y_ref, ...), custom_call_target="tpu_custom_call" | custom-call | tf_op jit(solution)/shard_map/project/pallas_call | solution.py:138
  100.0 0.0 copy-start.7
  100.0 1.3 slice.3.wx_ref
  101.3 10.4 %collective-permute-start.11 = (bf16[3072,128]{1,0:T(8,128)(2,1)S(1)}, bf16[3072,128]{1,0:T(8,128)(2,1)S(1)}, u32[]{:S(2)}, u32[]{:S(2)}) collective-permute-start(bf16[3072,128]{1,0:T(8,128)(2,1)S(1)} %slice.3.wx_ref), channel_id=1, source_target_pairs={{0,8},{8,0},{1,9},{9,1},{2,10},{10,2},{3,11},{11,3},{4,12},{12,4},... | collective-permute-start | bytes 2359304 | tf_op jit(solution)/shard_map/ppermute | solution.py:249
  111.7 0.0 copy-done
  111.7 2.6 %collective-permute-start.6 = (bf16[768,256]{1,0:T(8,128)(2,1)S(1)}, bf16[768,256]{1,0:T(8,128)(2,1)S(1)}, u32[]{:S(2)}, u32[]{:S(2)}) collective-permute-start(bf16[768,256]{1,0:T(8,128)(2,1)S(1)} %copy-done), channel_id=1, source_target_pairs={{0,16},{16,32},{32,48},{48,64},{64,80},{80,96},{96,112},{112,128},... | collective-permute-start | bytes 1179656 | tf_op jit(solution)/shard_map/ppermute | solution.py:262
  114.3 0.0 copy-done.1
  114.3 6.3 %collective-permute-start.7 = (bf16[768,256]{1,0:T(8,128)(2,1)S(1)}, bf16[768,256]{1,0:T(8,128)(2,1)S(1)}, u32[]{:S(2)}, u32[]{:S(2)}) collective-permute-start(bf16[768,256]{1,0:T(8,128)(2,1)S(1)} %copy-done.1), channel_id=1, source_target_pairs={{0,496},{16,0},{32,16},{48,32},{64,48},{80,64},{96,80},{112,96},{1... | collective-permute-start | bytes 1179656 | tf_op jit(solution)/shard_map/ppermute | solution.py:262
  120.6 1.9 %collective-permute-start.8 = (bf16[256,256]{1,0:T(8,128)(2,1)S(1)}, bf16[256,256]{1,0:T(8,128)(2,1)S(1)}, u32[]{:S(2)}, u32[]{:S(2)}) collective-permute-start(bf16[256,256]{1,0:T(8,128)(2,1)S(1)} %copy-done.7), channel_id=1, source_target_pairs={{0,32},{16,48},{32,64},{48,80},{64,96},{80,112},{96,128},{112,144}... | collective-permute-start | bytes 393224 | tf_op jit(solution)/shard_map/ppermute | solution.py:262
  122.6 5.5 %collective-permute-start.9 = (bf16[256,256]{1,0:T(8,128)(2,1)S(1)}, bf16[256,256]{1,0:T(8,128)(2,1)S(1)}, u32[]{:S(2)}, u32[]{:S(2)}) collective-permute-start(bf16[256,256]{1,0:T(8,128)(2,1)S(1)} %copy-done.6), channel_id=1, source_target_pairs={{0,224},{16,240},{32,0},{48,16},{64,32},{80,48},{96,64},{112,80},{... | collective-permute-start | bytes 393224 | tf_op jit(solution)/shard_map/ppermute | solution.py:262
  128.0 1.7 collective-permute-done.8.low_ref
  129.8 4.6 %collective-permute-done.9.high_ref = bf16[256,256]{1,0:T(8,128)(2,1)S(1)} collective-permute-done((bf16[256,256]{1,0:T(8,128)(2,1)S(1)}, bf16[256,256]{1,0:T(8,128)(2,1)S(1)}, u32[]{:S(2)}, u32[]{:S(2)}) %collective-permute-start.9) | collective-permute-done | bytes 131104 | tf_op jit(solution)/shard_map/ppermute | solution.py:262
  134.4 0.0 collective-permute-done.6.before_ref
  134.4 0.0 collective-permute-done.7.after_ref
  134.4 2.3 %shard_map.74 = bf16[256,128]{1,0:T(8,128)(2,1)S(1)} custom-call(s32[1]{0:T(128)} %bitcast.me_ref, s32[1,1]{1,0:T(1,128)} %collective-permute-done.5.flag_ref, bf16[2,256,128]{2,1,0:T(8,128)(2,1)S(1)} %copy-done.2, bf16[768,256]{1,0:T(8,128)(2,1)S(1)} %copy-done, bf16[768,256]{1,0:T(8,128)(2,1)S(1)} %copy-done.1, ...), custom_call_target="tpu_custom_call" | custom-call | flops 369098752 | bytes 2097152 | tf_op jit(solution)/shard_map/pallas_call | solution.py:208
  136.7 3.1 %collective-permute-start.10 = (bf16[256,128]{1,0:T(8,128)(2,1)S(1)}, bf16[256,128]{1,0:T(8,128)(2,1)S(1)}, u32[]{:S(2)}, u32[]{:S(2)}) collective-permute-start(bf16[256,128]{1,0:T(8,128)(2,1)S(1)} %shard_map.74), channel_id=1, source_target_pairs={{0,8},{8,0},{1,9},{9,1},{2,10},{10,2},{3,11},{11,3},{4,12},{12,4},... | collective-permute-start | bytes 196616 | tf_op jit(solution)/shard_map/ppermute | solution.py:249
  140.4 1.7 shard_map.73.ax_ref
  142.1 0.0 collective-permute-done.10.ay_ref
  142.1 0.0 collective-permute-done.11.wy_ref
  142.1 0.7 mix.1
  142.8 25.9 %all_to_all.21 = bf16[8,256,384]{2,1,0:T(8,128)(2,1)S(1)} all-to-all(bf16[8,256,384]{2,1,0:T(8,128)(2,1)S(1)} %mix.1), channel_id=1, replica_groups=mesh['x_hi'=2,'z_hi'=4,'z_lo'=4,'core'=2,'y'=4,'x_lo'=2] {'y','x_lo'}, dimensions={0} | all-to-all | bytes 3145728 | tf_op jit(solution)/shard_map/all_to_all | solution.py:292
  168.7 0.9 reduce_sum.12
  (11 shorter events, 0.0 us)
Async XLA Ops:
  6.5 86.3 %all-gather.2.cloned.1.call-start = ((), (), s32[]{:S(2)}) async-start(), calls=%async_computation.4 | async-start | bytes 3342336 | tf_op jit(solution)/shard_map/all_gather | solution.py:255
  27.3 3.7 %copy-start.5 = (bf16[32,384]{1,0:T(8,128)(2,1)S(1)}, bf16[32,384]{1,0:T(8,128)(2,1)}, u32[]{:S(2)}) copy-start(bf16[32,384]{1,0:T(8,128)(2,1)} %param.8) | copy-start | bytes 73732
  27.3 28.9 %all-to-all-start.1 = ((bf16[8,256,384]{2,1,0:T(8,128)(2,1)}), bf16[8,256,384]{2,1,0:T(8,128)(2,1)S(1)}, u32[]{:S(2)}, u32[]{:S(2)}) async-start(bf16[8,256,384]{2,1,0:T(8,128)(2,1)} %broadcast_in_dim.4), calls=%async_computation.1 | async-start | bytes 3145728 | tf_op jit(solution)/shard_map/all_to_all | solution.py:23
  31.1 20.8 %collective-permute-start.1 = (bf16[32,384]{1,0:T(8,128)(2,1)S(1)}, bf16[32,384]{1,0:T(8,128)(2,1)S(1)}, u32[]{:S(2)}, u32[]{:S(2)}) collective-permute-start(bf16[32,384]{1,0:T(8,128)(2,1)S(1)} %copy-done.5), channel_id=1, source_target_pairs={{0,64},{16,80},{32,96},{48,112},{64,128},{80,144},{96,160},{112,17... | collective-permute-start | bytes 73736 | tf_op jit(solution)/shard_map/ppermute | solution.py:262
  36.1 15.8 %collective-permute-start.2 = (bf16[32,384]{1,0:T(8,128)(2,1)S(1)}, bf16[32,384]{1,0:T(8,128)(2,1)S(1)}, u32[]{:S(2)}, u32[]{:S(2)}) collective-permute-start(bf16[32,384]{1,0:T(8,128)(2,1)S(1)} %copy-done.5), channel_id=1, source_target_pairs={{0,128},{16,144},{32,160},{48,176},{64,192},{80,208},{96,224},{112... | collective-permute-start | bytes 73736 | tf_op jit(solution)/shard_map/ppermute | solution.py:262
  46.7 9.5 %collective-permute-start.3 = (bf16[32,384]{1,0:T(8,128)(2,1)S(1)}, bf16[32,384]{1,0:T(8,128)(2,1)S(1)}, u32[]{:S(2)}, u32[]{:S(2)}) collective-permute-start(bf16[32,384]{1,0:T(8,128)(2,1)S(1)} %copy-done.5), channel_id=1, source_target_pairs={{0,192},{16,208},{32,224},{48,240},{64,0},{80,16},{96,32},{112,48}... | collective-permute-start | bytes 73736 | tf_op jit(solution)/shard_map/ppermute | solution.py:262
  56.2 6.5 %copy-start.3 = (bf16[8,256,384]{2,1,0:T(8,128)(2,1)}, bf16[8,256,384]{2,1,0:T(8,128)(2,1)S(1)}, u32[]{:S(2)}) copy-start(bf16[8,256,384]{2,1,0:T(8,128)(2,1)S(1)} %all-to-all-done.1.x_ref) | copy-start | bytes 4718596
  57.7 24.6 %all-to-all-start.2 = ((bf16[16,128,384]{2,1,0:T(8,128)(2,1)}), bf16[16,128,384]{2,1,0:T(8,128)(2,1)S(1)}, u32[]{:S(2)}, u32[]{:S(2)}) async-start(bf16[16,128,384]{2,1,0:T(8,128)(2,1)} %broadcast_in_dim.5), calls=%async_computation.2 | async-start | bytes 3145728 | tf_op jit(solution)/shard_map/all_to_all | solution.py:23
  62.8 29.0 %collective-permute-start = (bf16[8,256,384]{2,1,0:T(8,128)(2,1)S(1)}, bf16[8,256,384]{2,1,0:T(8,128)(2,1)}, u32[]{:S(2)}, u32[]{:S(2)}) collective-permute-start(bf16[8,256,384]{2,1,0:T(8,128)(2,1)S(1)} %all-to-all-done.1.x_ref), channel_id=1, source_target_pairs={{0,8},{8,0},{1,9},{9,1},{2,10},{10,2},{3,11},{11,3},{4,12},{12,4},... | collective-permute-start | bytes 4718600 | tf_op jit(solution)/shard_map/ppermute | solution.py:249
  82.4 10.5 %copy-start.4 = (bf16[16,128,384]{2,1,0:T(8,128)(2,1)}, bf16[16,128,384]{2,1,0:T(8,128)(2,1)S(1)}, u32[]{:S(2)}) copy-start(bf16[16,128,384]{2,1,0:T(8,128)(2,1)S(1)} %all-to-all-done.2) | copy-start | bytes 4718596
  82.4 9.4 %collective-permute-start.4 = (bf16[2,8,128,384]{3,2,1,0:T(8,128)(2,1)S(1)}, bf16[2,8,128,384]{3,2,1,0:T(8,128)(2,1)}, u32[]{:S(2)}, u32[]{:S(2)}) collective-permute-start(bf16[2,8,128,384]{3,2,1,0:T(8,128)(2,1)S(1)} %bitcast.7), channel_id=1, source_target_pairs={{0,8},{8,0},{1,9},{9,1},{2,10},{10,2},{3,11},{11,3},{4,12},{12,4},... | collective-permute-start | bytes 4718600 | tf_op jit(solution)/shard_map/ppermute | solution.py:249
  88.6 3.2 %collective-permute-start.5 = (s32[1,1]{1,0:T(1,128)}, s32[1,1]{1,0:T(1,128)}, u32[]{:S(2)}, u32[]{:S(2)}) collective-permute-start(s32[1,1]{1,0:T(1,128)} %param.13), channel_id=1, source_target_pairs={{0,8},{8,0},{1,9},{9,1},{2,10},{10,2},{3,11},{11,3},{4,12},{12,4},... | collective-permute-start | bytes 20 | tf_op jit(solution)/shard_map/ppermute | solution.py:249
  100.0 11.7 %copy-start = (bf16[768,256]{1,0:T(8,128)(2,1)S(1)}, bf16[768,256]{1,0:T(8,128)(2,1)}, u32[]{:S(2)}) copy-start(bf16[768,256]{1,0:T(8,128)(2,1)} %get-tuple-element.31.forward_ref) | copy-start | bytes 1179652
  100.0 14.3 %copy-start.1 = (bf16[768,256]{1,0:T(8,128)(2,1)S(1)}, bf16[768,256]{1,0:T(8,128)(2,1)}, u32[]{:S(2)}) copy-start(bf16[768,256]{1,0:T(8,128)(2,1)} %get-tuple-element.32.backward_ref) | copy-start | bytes 1179652
  100.0 20.6 %copy-start.7 = (bf16[256,256]{1,0:T(8,128)(2,1)S(1)}, bf16[256,256]{1,0:T(8,128)(2,1)}, u32[]{:S(2)}) copy-start(bf16[256,256]{1,0:T(8,128)(2,1)} %get-tuple-element.33) | copy-start | bytes 393220
  100.0 22.6 %copy-start.6 = (bf16[256,256]{1,0:T(8,128)(2,1)S(1)}, bf16[256,256]{1,0:T(8,128)(2,1)}, u32[]{:S(2)}) copy-start(bf16[256,256]{1,0:T(8,128)(2,1)} %get-tuple-element.34) | copy-start | bytes 393220
  100.0 34.4 %copy-start.2 = (bf16[2,256,128]{2,1,0:T(8,128)(2,1)S(1)}, bf16[2,256,128]{2,1,0:T(8,128)(2,1)}, u32[]{:S(2)}) copy-start(bf16[2,256,128]{2,1,0:T(8,128)(2,1)} %get-tuple-element.30.q_ref) | copy-start | bytes 393220
  101.3 40.8 %collective-permute-start.11 = (bf16[3072,128]{1,0:T(8,128)(2,1)S(1)}, bf16[3072,128]{1,0:T(8,128)(2,1)S(1)}, u32[]{:S(2)}, u32[]{:S(2)}) collective-permute-start(bf16[3072,128]{1,0:T(8,128)(2,1)S(1)} %slice.3.wx_ref), channel_id=1, source_target_pairs={{0,8},{8,0},{1,9},{9,1},{2,10},{10,2},{3,11},{11,3},{4,12},{12,4},... | collective-permute-start | bytes 2359304 | tf_op jit(solution)/shard_map/ppermute | solution.py:249
  111.7 22.7 %collective-permute-start.6 = (bf16[768,256]{1,0:T(8,128)(2,1)S(1)}, bf16[768,256]{1,0:T(8,128)(2,1)S(1)}, u32[]{:S(2)}, u32[]{:S(2)}) collective-permute-start(bf16[768,256]{1,0:T(8,128)(2,1)S(1)} %copy-done), channel_id=1, source_target_pairs={{0,16},{16,32},{32,48},{48,64},{64,80},{80,96},{96,112},{112,128},... | collective-permute-start | bytes 1179656 | tf_op jit(solution)/shard_map/ppermute | solution.py:262
  114.3 20.1 %collective-permute-start.7 = (bf16[768,256]{1,0:T(8,128)(2,1)S(1)}, bf16[768,256]{1,0:T(8,128)(2,1)S(1)}, u32[]{:S(2)}, u32[]{:S(2)}) collective-permute-start(bf16[768,256]{1,0:T(8,128)(2,1)S(1)} %copy-done.1), channel_id=1, source_target_pairs={{0,496},{16,0},{32,16},{48,32},{64,48},{80,64},{96,80},{112,96},{1... | collective-permute-start | bytes 1179656 | tf_op jit(solution)/shard_map/ppermute | solution.py:262
  120.6 9.2 %collective-permute-start.8 = (bf16[256,256]{1,0:T(8,128)(2,1)S(1)}, bf16[256,256]{1,0:T(8,128)(2,1)S(1)}, u32[]{:S(2)}, u32[]{:S(2)}) collective-permute-start(bf16[256,256]{1,0:T(8,128)(2,1)S(1)} %copy-done.7), channel_id=1, source_target_pairs={{0,32},{16,48},{32,64},{48,80},{64,96},{80,112},{96,128},{112,144}... | collective-permute-start | bytes 393224 | tf_op jit(solution)/shard_map/ppermute | solution.py:262
  122.6 11.8 %collective-permute-start.9 = (bf16[256,256]{1,0:T(8,128)(2,1)S(1)}, bf16[256,256]{1,0:T(8,128)(2,1)S(1)}, u32[]{:S(2)}, u32[]{:S(2)}) collective-permute-start(bf16[256,256]{1,0:T(8,128)(2,1)S(1)} %copy-done.6), channel_id=1, source_target_pairs={{0,224},{16,240},{32,0},{48,16},{64,32},{80,48},{96,64},{112,80},{... | collective-permute-start | bytes 393224 | tf_op jit(solution)/shard_map/ppermute | solution.py:262
  136.7 5.4 %collective-permute-start.10 = (bf16[256,128]{1,0:T(8,128)(2,1)S(1)}, bf16[256,128]{1,0:T(8,128)(2,1)S(1)}, u32[]{:S(2)}, u32[]{:S(2)}) collective-permute-start(bf16[256,128]{1,0:T(8,128)(2,1)S(1)} %shard_map.74), channel_id=1, source_target_pairs={{0,8},{8,0},{1,9},{9,1},{2,10},{10,2},{3,11},{11,3},{4,12},{12,4},... | collective-permute-start | bytes 196616 | tf_op jit(solution)/shard_map/ppermute | solution.py:249
Sparse Core Ops, SparseCore 0:
  25.2 67.5 all-gather.1
where the time goes:
time: 177 us; the launch traced here: 176 us
  starting transfers between devices  72.6 us (41%)
  blocking collectives  42.8 us (24%)
  waiting for transfers between devices  27.4 us (15%)
  between operations  14.3 us (8%)
  Pallas kernels  13.4 us (8%)
  local copies, waits for them, and re-layouts  5.04 us (3%)
    ppermute x7, starting transfers between devices, shift(): lax.ppermute(block, axes, [(i, (i + by) % count) for i in range(count)])  37.1 us
    ppermute x5, starting transfers between devices, swap(): return lax.ppermute(block, 'core', [(0, 1), (1, 0)])  26.8 us
    all_to_all x1, blocking collectives, local(): shares = lax.all_to_all(shares, TP, 0, 0, tiled=True)  25.9 us
    all_to_all x1, blocking collectives, local(): plane = lax.all_to_all(mine, ('x_hi', 'core'), 0, 0, tiled=True)  17 us
    all_to_all x2, waiting for transfers between devices, spread(): lax.all_to_all(jnp.broadcast_to(block[None], (count,) + block.shape), axe...  14.4 us
    ppermute x7, waiting for transfers between devices, shift(): lax.ppermute(block, axes, [(i, (i + by) % count) for i in range(count)])  10.6 us
    all_to_all x2, starting transfers between devices, spread(): lax.all_to_all(jnp.broadcast_to(block[None], (count,) + block.shape), axe...  8.72 us
    pallas_call x1, Pallas kernels, project(): pl.pallas_call(project_kernel, in_specs=[pl.BlockSpec(memory_space=pltpu....  7.1 us
  transfers between devices with their start and end apart: 15, of which 6 were waited for; matrix products, arithmetic and copies ran while one was open for 2% of the time, Pallas kernels for 2%

commit v1 on v0

--- a/solution.py
+++ b/solution.py
@@ -60,8 +60,7 @@
     kg_ref,
     forward_ref,
     backward_ref,
-    low_ref,
-    high_ref,
+    far_ref,
     q_ref,
     acc,
     qacc,
@@ -106,16 +105,11 @@
         )
 
     kg, qg = kg_ref[...], qg_ref[...]
-    for half, part_ref in enumerate((low_ref, high_ref)):
-        lines = pl.ds(half * far // 2, far // 2)
-        source = pl.ds(2 * count + half * far // 2, far // 2)
-        k = unit(acc[source, :HEAD], kg).astype(BF16)
-        v = acc[source, HEAD:].astype(BF16)
-        for out_ref in (forward_ref, backward_ref):
-            out_ref[lines, :HEAD] = k
-            out_ref[lines, HEAD:] = v
-        part_ref[:, :HEAD] = k
-        part_ref[:, HEAD:] = v
+    k = unit(acc[pl.ds(2 * count, far), :HEAD], kg).astype(BF16)
+    v = acc[pl.ds(2 * count, far), HEAD:].astype(BF16)
+    for out_ref in (forward_ref, backward_ref, far_ref):
+        out_ref[pl.ds(0, far), :HEAD] = k
+        out_ref[pl.ds(0, far), HEAD:] = v
     me = me_ref[0]
     lines = pl.ds(far, count)
     for slab, out_ref in enumerate((backward_ref, forward_ref)):
@@ -132,7 +126,7 @@
     steps = parts // pieces
     far = 2 * groups * rows
     total = 2 * count + far
-    shapes = [(far + count, 2 * HEAD)] * 2 + [(far // 2, 2 * HEAD)] * 2 + [(2, count, HEAD)]
+    shapes = [(far + count, 2 * HEAD)] * 2 + [(far, 2 * HEAD), (2, count, HEAD)]
     vmem = pl.BlockSpec(memory_space=pltpu.VMEM)
     hbm = pl.BlockSpec(memory_space=pltpu.HBM)
     return pl.pallas_call(
@@ -164,8 +158,7 @@
     backward_ref,
     before_ref,
     after_ref,
-    low_ref,
-    high_ref,
+    far_ref,
     o_ref,
     near,
 ):
@@ -187,7 +180,7 @@
     scale = 1.0 / math.sqrt(HEAD)
     q = q_ref[slab]
     lines = pl.ds(0, style)
-    refs = [near, *(r.at[lines] for r in (forward_ref, before_ref, after_ref)), low_ref, high_ref]
+    refs = [near, *(r.at[lines] for r in (forward_ref, before_ref, after_ref)), far_ref]
     scores = []
     for n, ref in enumerate(refs):
         part = lax.dot_general(q, ref[:, :HEAD], NT, preferred_element_type=F32) * scale
@@ -273,19 +266,21 @@
     flags = (attend_flags, swap(attend_flags))
     slabs, styles, flags = lax.optimization_barrier((slabs, styles, flags))
 
-    forward, backward, low, high, query = project(
+    forward, backward, far, query = project(
         me, slabs, styles, panel, query_gain.reshape(1, HEAD), key_gain.reshape(1, HEAD)
     )
     chips = halves * rows
     before = shift(forward, ("x_hi",) + Z, chips, 1)
     after = shift(backward, ("x_hi",) + Z, chips, -1)
-    low = shift(low, Z, rows, 2)
-    high = shift(high, Z, rows, -2)
+    pairs = [
+        (i * cores + c, (i + 2 - 4 * c) % rows * cores + c) for i in range(rows) for c in (0, 1)
+    ]
+    far = lax.ppermute(far, Z + ("core",), pairs)
     panel, query = lax.optimization_barrier((panel, query))
     out_own = panel[:, 3 * HEAD :]
     out_other = swap(out_own)
 
-    keys = (forward, backward, before, after, low, high)
+    keys = (forward, backward, before, after, far)
     theirs = swap(attend(1, me, flags[1], query, *keys))
     mine = attend(0, me, flags[0], query, *keys)
     shares = mix((mine, theirs), (out_own, out_other), parts)

time: 177 us -> 177 us (level)
  starting transfers between devices: 72.6 us -> 65.8 us
  waiting for transfers between devices: 27.4 us -> 33.8 us
    ppermute x0 -> x1, waiting for transfers between devices: none -> 12.6 us  [local(): far = lax.ppermute(far, Z + ('core',), pairs)]
    ppermute x7 -> x5, starting transfers between devices: 37.1 us -> 29.7 us  [shift(): lax.ppermute(block, axes, [(i, (i + by) % count) for i in range(count)])]
    ppermute x7 -> x5, waiting for transfers between devices: 10.6 us -> 4.32 us  [shift(): lax.ppermute(block, axes, [(i, (i + by) % count) for i in range(count)])]
    ppermute x0 -> x1, starting transfers between devices: none -> 1.92 us  [local(): far = lax.ppermute(far, Z + ('core',), pairs)]
  transfers between devices with their start and end apart: 15 -> 14, of which waited for: 6 -> 5; matrix products, arithmetic and copies ran while one was open for 2% -> 2% of each run, Pallas kernels for 2% -> 2%
where the time goes in v1:
time: 177 us; the launch traced here: 175 us
  starting transfers between devices  65.8 us (37%)
  blocking collectives  42.3 us (24%)
  waiting for transfers between devices  33.8 us (19%)
  between operations  14.3 us (8%)
  Pallas kernels  13.3 us (8%)
  local copies, waits for them, and re-layouts  5.04 us (3%)
    ppermute x5, starting transfers between devices, shift(): lax.ppermute(block, axes, [(i, (i + by) % count) for i in range(count)])  29.7 us
    ppermute x5, starting transfers between devices, swap(): return lax.ppermute(block, 'core', [(0, 1), (1, 0)])  25.4 us
    all_to_all x1, blocking collectives, local(): shares = lax.all_to_all(shares, TP, 0, 0, tiled=True)  25.3 us
    all_to_all x1, blocking collectives, local(): plane = lax.all_to_all(mine, ('x_hi', 'core'), 0, 0, tiled=True)  17 us
    all_to_all x2, waiting for transfers between devices, spread(): lax.all_to_all(jnp.broadcast_to(block[None], (count,) + block.shape), axe...  14.6 us
    ppermute x1, waiting for transfers between devices, local(): far = lax.ppermute(far, Z + ('core',), pairs)  12.6 us
    all_to_all x2, starting transfers between devices, spread(): lax.all_to_all(jnp.broadcast_to(block[None], (count,) + block.shape), axe...  8.72 us
    pallas_call x1, Pallas kernels, project(): pl.pallas_call(project_kernel, in_specs=[pl.BlockSpec(memory_space=pltpu....  7.12 us
  transfers between devices with their start and end apart: 14, of which 5 were waited for; matrix products, arithmetic and copies ran while one was open for 2% of the time, Pallas kernels for 2%

profile of v1, /device:TPU:1, one launch (start us, length us, event | category | flops | bytes accessed | tf_op | source)
XLA Modules:
  0.0 175.5 jit_solution(4827695307422671681)
XLA Ops:
  6.5 0.0 all-gather.2.cloned.1.call-start
  6.5 1.6 pack.1
  8.1 17.0 %all_to_all.20 = bf16[4,48,512]{2,1,0:T(8,128)(2,1)} all-to-all(bf16[4,48,512]{2,1,0:T(8,128)(2,1)} %pack.1), channel_id=1, replica_groups=mesh['x_hi'=2,'z_hi'=4,'z_lo'=4,'core'=2,'y'=4,'x_lo'=2] {'x_hi','core'}, dimensions={0} | all-to-all | bytes 393216 | tf_op jit(solution)/shard_map/all_to_all | solution.py:246
  25.1 0.0 all-gather.2.cloned.1.call-update
  25.1 2.2 %broadcast_in_dim.4 = bf16[8,256,384]{2,1,0:T(8,128)(2,1)} broadcast(bf16[256,384]{1,0:T(8,128)(2,1)} %param.7), dimensions={1,2} | broadcast | bytes 1769472 | tf_op jit(solution)/shard_map/broadcast_in_dim | solution.py:24
  27.3 3.7 %all-to-all-start.1 = ((bf16[8,256,384]{2,1,0:T(8,128)(2,1)}), bf16[8,256,384]{2,1,0:T(8,128)(2,1)S(1)}, u32[]{:S(2)}, u32[]{:S(2)}) async-start(bf16[8,256,384]{2,1,0:T(8,128)(2,1)} %broadcast_in_dim.4), calls=%async_computation.1 | async-start | bytes 3145728 | tf_op jit(solution)/shard_map/all_to_all | solution.py:23
  31.0 0.0 copy-done.5
  31.1 5.0 %collective-permute-start.1 = (bf16[32,384]{1,0:T(8,128)(2,1)S(1)}, bf16[32,384]{1,0:T(8,128)(2,1)S(1)}, u32[]{:S(2)}, u32[]{:S(2)}) collective-permute-start(bf16[32,384]{1,0:T(8,128)(2,1)S(1)} %copy-done.5), channel_id=1, source_target_pairs={{0,64},{16,80},{32,96},{48,112},{64,128},{80,144},{96,160},{112,17... | collective-permute-start | bytes 73736 | tf_op jit(solution)/shard_map/ppermute | solution.py:255
  36.1 10.6 %collective-permute-start.2 = (bf16[32,384]{1,0:T(8,128)(2,1)S(1)}, bf16[32,384]{1,0:T(8,128)(2,1)S(1)}, u32[]{:S(2)}, u32[]{:S(2)}) collective-permute-start(bf16[32,384]{1,0:T(8,128)(2,1)S(1)} %copy-done.5), channel_id=1, source_target_pairs={{0,128},{16,144},{32,160},{48,176},{64,192},{80,208},{96,224},{112... | collective-permute-start | bytes 73736 | tf_op jit(solution)/shard_map/ppermute | solution.py:255
  46.7 5.2 %collective-permute-start.3 = (bf16[32,384]{1,0:T(8,128)(2,1)S(1)}, bf16[32,384]{1,0:T(8,128)(2,1)S(1)}, u32[]{:S(2)}, u32[]{:S(2)}) collective-permute-start(bf16[32,384]{1,0:T(8,128)(2,1)S(1)} %copy-done.5), channel_id=1, source_target_pairs={{0,192},{16,208},{32,224},{48,240},{64,0},{80,16},{96,32},{112,48}... | collective-permute-start | bytes 73736 | tf_op jit(solution)/shard_map/ppermute | solution.py:255
  51.9 0.0 collective-permute-done.1
  51.9 0.0 collective-permute-done.2
  51.9 4.3 %collective-permute-done.3 = bf16[32,384]{1,0:T(8,128)(2,1)S(1)} collective-permute-done((bf16[32,384]{1,0:T(8,128)(2,1)S(1)}, bf16[32,384]{1,0:T(8,128)(2,1)S(1)}, u32[]{:S(2)}, u32[]{:S(2)}) %collective-permute-start.3) | collective-permute-done | bytes 24608 | tf_op jit(solution)/shard_map/ppermute | solution.py:255
  56.2 0.0 all-to-all-done.1.x_ref
  56.2 0.0 copy-start.3
  56.3 1.5 broadcast_in_dim.5
  57.8 5.0 %all-to-all-start.2 = ((bf16[16,128,384]{2,1,0:T(8,128)(2,1)}), bf16[16,128,384]{2,1,0:T(8,128)(2,1)S(1)}, u32[]{:S(2)}, u32[]{:S(2)}) async-start(bf16[16,128,384]{2,1,0:T(8,128)(2,1)} %broadcast_in_dim.5), calls=%async_computation.2 | async-start | bytes 3145728 | tf_op jit(solution)/shard_map/all_to_all | solution.py:23
  62.8 0.0 copy-done.3
  62.8 5.1 %collective-permute-start = (bf16[8,256,384]{2,1,0:T(8,128)(2,1)S(1)}, bf16[8,256,384]{2,1,0:T(8,128)(2,1)}, u32[]{:S(2)}, u32[]{:S(2)}) collective-permute-start(bf16[8,256,384]{2,1,0:T(8,128)(2,1)S(1)} %all-to-all-done.1.x_ref), channel_id=1, source_target_pairs={{0,8},{8,0},{1,9},{9,1},{2,10},{10,2},{3,11},{11,3},{4,12},{12,4},... | collective-permute-start | bytes 4718600 | tf_op jit(solution)/shard_map/ppermute | solution.py:242
  67.9 14.6 %all-to-all-done.2 = bf16[16,128,384]{2,1,0:T(8,128)(2,1)S(1)} async-done(((bf16[16,128,384]{2,1,0:T(8,128)(2,1)}), bf16[16,128,384]{2,1,0:T(8,128)(2,1)S(1)}, u32[]{:S(2)}, u32[]{:S(2)}) %all-to-all-start.2) | async-done | bytes 1572896 | tf_op jit(solution)/shard_map/all_to_all | solution.py:23
  82.5 6.1 %collective-permute-start.4 = (bf16[2,8,128,384]{3,2,1,0:T(8,128)(2,1)S(1)}, bf16[2,8,128,384]{3,2,1,0:T(8,128)(2,1)}, u32[]{:S(2)}, u32[]{:S(2)}) collective-permute-start(bf16[2,8,128,384]{3,2,1,0:T(8,128)(2,1)S(1)} %bitcast.7), channel_id=1, source_target_pairs={{0,8},{8,0},{1,9},{9,1},{2,10},{10,2},{3,11},{11,3},{4,12},{12,4},... | collective-permute-start | bytes 4718600 | tf_op jit(solution)/shard_map/ppermute | solution.py:242
  88.7 1.9 %collective-permute-start.5 = (s32[1,1]{1,0:T(1,128)}, s32[1,1]{1,0:T(1,128)}, u32[]{:S(2)}, u32[]{:S(2)}) collective-permute-start(s32[1,1]{1,0:T(1,128)} %param.13), channel_id=1, source_target_pairs={{0,8},{8,0},{1,9},{9,1},{2,10},{10,2},{3,11},{11,3},{4,12},{12,4},... | collective-permute-start | bytes 20 | tf_op jit(solution)/shard_map/ppermute | solution.py:242
  90.6 1.4 collective-permute-done.5.flag_ref
  92.0 0.0 collective-permute-done.y_ref
  92.0 0.0 collective-permute-done.4.sy_ref
  92.0 0.9 all-gather.2.cloned.1.call-done
  92.9 7.1 %project.1 = (bf16[768,256]{1,0:T(8,128)(2,1)}, bf16[768,256]{1,0:T(8,128)(2,1)}, bf16[512,256]{1,0:T(8,128)(2,1)}, bf16[2,256,128]{2,1,0:T(8,128)(2,1)}) custom-call(s32[1]{0:T(128)} %bitcast.me_ref, bf16[8,256,384]{2,1,0:T(8,128)(2,1)} %copy-done.3, bf16[8,256,384]{2,1,0:T(8,128)(2,1)} %collective-permute-done.y_ref, bf16[2,8,128,384]{3,2,1,0:T(8,128)(2,1)} %bitcast.8, ...), custom_call_target="tpu_custom_call" | custom-call | tf_op jit(solution)/shard_map/project/pallas_call | solution.py:132
  100.0 0.0 copy-start
  100.0 0.0 copy-start.1
  100.0 0.0 copy-start.6
  100.0 0.0 copy-start.2
  100.1 1.3 slice.3.wx_ref
  101.3 10.3 %collective-permute-start.10 = (bf16[3072,128]{1,0:T(8,128)(2,1)S(1)}, bf16[3072,128]{1,0:T(8,128)(2,1)S(1)}, u32[]{:S(2)}, u32[]{:S(2)}) collective-permute-start(bf16[3072,128]{1,0:T(8,128)(2,1)S(1)} %slice.3.wx_ref), channel_id=1, source_target_pairs={{0,8},{8,0},{1,9},{9,1},{2,10},{10,2},{3,11},{11,3},{4,12},{12,4},... | collective-permute-start | bytes 2359304 | tf_op jit(solution)/shard_map/ppermute | solution.py:242
  111.7 2.6 %collective-permute-start.6 = (bf16[768,256]{1,0:T(8,128)(2,1)S(1)}, bf16[768,256]{1,0:T(8,128)(2,1)S(1)}, u32[]{:S(2)}, u32[]{:S(2)}) collective-permute-start(bf16[768,256]{1,0:T(8,128)(2,1)S(1)} %copy-done), channel_id=1, source_target_pairs={{0,16},{16,32},{32,48},{48,64},{64,80},{80,96},{96,112},{112,128},... | collective-permute-start | bytes 1179656 | tf_op jit(solution)/shard_map/ppermute | solution.py:255
  114.3 6.3 %collective-permute-start.7 = (bf16[768,256]{1,0:T(8,128)(2,1)S(1)}, bf16[768,256]{1,0:T(8,128)(2,1)S(1)}, u32[]{:S(2)}, u32[]{:S(2)}) collective-permute-start(bf16[768,256]{1,0:T(8,128)(2,1)S(1)} %copy-done.1), channel_id=1, source_target_pairs={{0,496},{16,0},{32,16},{48,32},{64,48},{80,64},{96,80},{112,96},{1... | collective-permute-start | bytes 1179656 | tf_op jit(solution)/shard_map/ppermute | solution.py:255
  120.6 0.0 copy-done.6
  120.6 1.9 %collective-permute-start.8 = (bf16[512,256]{1,0:T(8,128)(2,1)S(1)}, bf16[512,256]{1,0:T(8,128)(2,1)S(1)}, u32[]{:S(2)}, u32[]{:S(2)}) collective-permute-start(bf16[512,256]{1,0:T(8,128)(2,1)S(1)} %copy-done.6), channel_id=1, source_target_pairs={{0,32},{8,232},{16,48},{24,248},{32,64},{40,8},{48,80},{56,24},{64... | collective-permute-start | bytes 786440 | tf_op jit(solution)/shard_map/ppermute | solution.py:278
  122.5 12.6 %collective-permute-done.8.far_ref = bf16[512,256]{1,0:T(8,128)(2,1)S(1)} collective-permute-done((bf16[512,256]{1,0:T(8,128)(2,1)S(1)}, bf16[512,256]{1,0:T(8,128)(2,1)S(1)}, u32[]{:S(2)}, u32[]{:S(2)}) %collective-permute-start.8) | collective-permute-done | bytes 262176 | tf_op jit(solution)/shard_map/ppermute | solution.py:278
  135.1 0.0 collective-permute-done.6.before_ref
  135.1 0.0 collective-permute-done.7.after_ref
  135.1 2.3 %shard_map.74 = bf16[256,128]{1,0:T(8,128)(2,1)S(1)} custom-call(s32[1]{0:T(128)} %bitcast.me_ref, s32[1,1]{1,0:T(1,128)} %collective-permute-done.5.flag_ref, bf16[2,256,128]{2,1,0:T(8,128)(2,1)S(1)} %copy-done.2, bf16[768,256]{1,0:T(8,128)(2,1)S(1)} %copy-done, bf16[768,256]{1,0:T(8,128)(2,1)S(1)} %copy-done.1, ...), custom_call_target="tpu_custom_call" | custom-call | flops 369098752 | bytes 2097152 | tf_op jit(solution)/shard_map/pallas_call | solution.py:201
  137.4 1.9 %collective-permute-start.9 = (bf16[256,128]{1,0:T(8,128)(2,1)S(1)}, bf16[256,128]{1,0:T(8,128)(2,1)S(1)}, u32[]{:S(2)}, u32[]{:S(2)}) collective-permute-start(bf16[256,128]{1,0:T(8,128)(2,1)S(1)} %shard_map.74), channel_id=1, source_target_pairs={{0,8},{8,0},{1,9},{9,1},{2,10},{10,2},{3,11},{11,3},{4,12},{12,4},... | collective-permute-start | bytes 196616 | tf_op jit(solution)/shard_map/ppermute | solution.py:242
  140.0 1.6 shard_map.73.ax_ref
  141.7 0.0 collective-permute-done.9.ay_ref
  141.7 0.0 collective-permute-done.10.wy_ref
  141.7 0.7 mix.1
  142.4 25.3 %all_to_all.21 = bf16[8,256,384]{2,1,0:T(8,128)(2,1)S(1)} all-to-all(bf16[8,256,384]{2,1,0:T(8,128)(2,1)S(1)} %mix.1), channel_id=1, replica_groups=mesh['x_hi'=2,'z_hi'=4,'z_lo'=4,'core'=2,'y'=4,'x_lo'=2] {'y','x_lo'}, dimensions={0} | all-to-all | bytes 3145728 | tf_op jit(solution)/shard_map/all_to_all | solution.py:287
  167.7 0.9 reduce_sum.12
  (7 shorter events, 0.0 us)
Async XLA Ops:
  6.5 86.3 %all-gather.2.cloned.1.call-start = ((), (), s32[]{:S(2)}) async-start(), calls=%async_computation.4 | async-start | bytes 3342336 | tf_op jit(solution)/shard_map/all_gather | solution.py:248
  27.3 3.7 %copy-start.5 = (bf16[32,384]{1,0:T(8,128)(2,1)S(1)}, bf16[32,384]{1,0:T(8,128)(2,1)}, u32[]{:S(2)}) copy-start(bf16[32,384]{1,0:T(8,128)(2,1)} %param.8) | copy-start | bytes 73732
  27.3 28.9 %all-to-all-start.1 = ((bf16[8,256,384]{2,1,0:T(8,128)(2,1)}), bf16[8,256,384]{2,1,0:T(8,128)(2,1)S(1)}, u32[]{:S(2)}, u32[]{:S(2)}) async-start(bf16[8,256,384]{2,1,0:T(8,128)(2,1)} %broadcast_in_dim.4), calls=%async_computation.1 | async-start | bytes 3145728 | tf_op jit(solution)/shard_map/all_to_all | solution.py:23
  31.1 20.8 %collective-permute-start.1 = (bf16[32,384]{1,0:T(8,128)(2,1)S(1)}, bf16[32,384]{1,0:T(8,128)(2,1)S(1)}, u32[]{:S(2)}, u32[]{:S(2)}) collective-permute-start(bf16[32,384]{1,0:T(8,128)(2,1)S(1)} %copy-done.5), channel_id=1, source_target_pairs={{0,64},{16,80},{32,96},{48,112},{64,128},{80,144},{96,160},{112,17... | collective-permute-start | bytes 73736 | tf_op jit(solution)/shard_map/ppermute | solution.py:255
  36.1 15.8 %collective-permute-start.2 = (bf16[32,384]{1,0:T(8,128)(2,1)S(1)}, bf16[32,384]{1,0:T(8,128)(2,1)S(1)}, u32[]{:S(2)}, u32[]{:S(2)}) collective-permute-start(bf16[32,384]{1,0:T(8,128)(2,1)S(1)} %copy-done.5), channel_id=1, source_target_pairs={{0,128},{16,144},{32,160},{48,176},{64,192},{80,208},{96,224},{112... | collective-permute-start | bytes 73736 | tf_op jit(solution)/shard_map/ppermute | solution.py:255
  46.7 9.5 %collective-permute-start.3 = (bf16[32,384]{1,0:T(8,128)(2,1)S(1)}, bf16[32,384]{1,0:T(8,128)(2,1)S(1)}, u32[]{:S(2)}, u32[]{:S(2)}) collective-permute-start(bf16[32,384]{1,0:T(8,128)(2,1)S(1)} %copy-done.5), channel_id=1, source_target_pairs={{0,192},{16,208},{32,224},{48,240},{64,0},{80,16},{96,32},{112,48}... | collective-permute-start | bytes 73736 | tf_op jit(solution)/shard_map/ppermute | solution.py:255
  56.2 6.5 %copy-start.3 = (bf16[8,256,384]{2,1,0:T(8,128)(2,1)}, bf16[8,256,384]{2,1,0:T(8,128)(2,1)S(1)}, u32[]{:S(2)}) copy-start(bf16[8,256,384]{2,1,0:T(8,128)(2,1)S(1)} %all-to-all-done.1.x_ref) | copy-start | bytes 4718596
  57.8 24.7 %all-to-all-start.2 = ((bf16[16,128,384]{2,1,0:T(8,128)(2,1)}), bf16[16,128,384]{2,1,0:T(8,128)(2,1)S(1)}, u32[]{:S(2)}, u32[]{:S(2)}) async-start(bf16[16,128,384]{2,1,0:T(8,128)(2,1)} %broadcast_in_dim.5), calls=%async_computation.2 | async-start | bytes 3145728 | tf_op jit(solution)/shard_map/all_to_all | solution.py:23
  62.8 29.2 %collective-permute-start = (bf16[8,256,384]{2,1,0:T(8,128)(2,1)S(1)}, bf16[8,256,384]{2,1,0:T(8,128)(2,1)}, u32[]{:S(2)}, u32[]{:S(2)}) collective-permute-start(bf16[8,256,384]{2,1,0:T(8,128)(2,1)S(1)} %all-to-all-done.1.x_ref), channel_id=1, source_target_pairs={{0,8},{8,0},{1,9},{9,1},{2,10},{10,2},{3,11},{11,3},{4,12},{12,4},... | collective-permute-start | bytes 4718600 | tf_op jit(solution)/shard_map/ppermute | solution.py:242
  82.5 10.4 %copy-start.4 = (bf16[16,128,384]{2,1,0:T(8,128)(2,1)}, bf16[16,128,384]{2,1,0:T(8,128)(2,1)S(1)}, u32[]{:S(2)}) copy-start(bf16[16,128,384]{2,1,0:T(8,128)(2,1)S(1)} %all-to-all-done.2) | copy-start | bytes 4718596
  82.5 9.5 %collective-permute-start.4 = (bf16[2,8,128,384]{3,2,1,0:T(8,128)(2,1)S(1)}, bf16[2,8,128,384]{3,2,1,0:T(8,128)(2,1)}, u32[]{:S(2)}, u32[]{:S(2)}) collective-permute-start(bf16[2,8,128,384]{3,2,1,0:T(8,128)(2,1)S(1)} %bitcast.7), channel_id=1, source_target_pairs={{0,8},{8,0},{1,9},{9,1},{2,10},{10,2},{3,11},{11,3},{4,12},{12,4},... | collective-permute-start | bytes 4718600 | tf_op jit(solution)/shard_map/ppermute | solution.py:242
  88.7 3.3 %collective-permute-start.5 = (s32[1,1]{1,0:T(1,128)}, s32[1,1]{1,0:T(1,128)}, u32[]{:S(2)}, u32[]{:S(2)}) collective-permute-start(s32[1,1]{1,0:T(1,128)} %param.13), channel_id=1, source_target_pairs={{0,8},{8,0},{1,9},{9,1},{2,10},{10,2},{3,11},{11,3},{4,12},{12,4},... | collective-permute-start | bytes 20 | tf_op jit(solution)/shard_map/ppermute | solution.py:242
  100.0 11.7 %copy-start = (bf16[768,256]{1,0:T(8,128)(2,1)S(1)}, bf16[768,256]{1,0:T(8,128)(2,1)}, u32[]{:S(2)}) copy-start(bf16[768,256]{1,0:T(8,128)(2,1)} %get-tuple-element.30.forward_ref) | copy-start | bytes 1179652
  100.0 14.3 %copy-start.1 = (bf16[768,256]{1,0:T(8,128)(2,1)S(1)}, bf16[768,256]{1,0:T(8,128)(2,1)}, u32[]{:S(2)}) copy-start(bf16[768,256]{1,0:T(8,128)(2,1)} %get-tuple-element.31.backward_ref) | copy-start | bytes 1179652
  100.0 20.6 %copy-start.6 = (bf16[512,256]{1,0:T(8,128)(2,1)S(1)}, bf16[512,256]{1,0:T(8,128)(2,1)}, u32[]{:S(2)}) copy-start(bf16[512,256]{1,0:T(8,128)(2,1)} %get-tuple-element.32) | copy-start | bytes 786436
  100.0 35.1 %copy-start.2 = (bf16[2,256,128]{2,1,0:T(8,128)(2,1)S(1)}, bf16[2,256,128]{2,1,0:T(8,128)(2,1)}, u32[]{:S(2)}) copy-start(bf16[2,256,128]{2,1,0:T(8,128)(2,1)} %get-tuple-element.29.q_ref) | copy-start | bytes 393220
  101.3 40.3 %collective-permute-start.10 = (bf16[3072,128]{1,0:T(8,128)(2,1)S(1)}, bf16[3072,128]{1,0:T(8,128)(2,1)S(1)}, u32[]{:S(2)}, u32[]{:S(2)}) collective-permute-start(bf16[3072,128]{1,0:T(8,128)(2,1)S(1)} %slice.3.wx_ref), channel_id=1, source_target_pairs={{0,8},{8,0},{1,9},{9,1},{2,10},{10,2},{3,11},{11,3},{4,12},{12,4},... | collective-permute-start | bytes 2359304 | tf_op jit(solution)/shard_map/ppermute | solution.py:242
  111.7 23.5 %collective-permute-start.6 = (bf16[768,256]{1,0:T(8,128)(2,1)S(1)}, bf16[768,256]{1,0:T(8,128)(2,1)S(1)}, u32[]{:S(2)}, u32[]{:S(2)}) collective-permute-start(bf16[768,256]{1,0:T(8,128)(2,1)S(1)} %copy-done), channel_id=1, source_target_pairs={{0,16},{16,32},{32,48},{48,64},{64,80},{80,96},{96,112},{112,128},... | collective-permute-start | bytes 1179656 | tf_op jit(solution)/shard_map/ppermute | solution.py:255
  114.3 20.9 %collective-permute-start.7 = (bf16[768,256]{1,0:T(8,128)(2,1)S(1)}, bf16[768,256]{1,0:T(8,128)(2,1)S(1)}, u32[]{:S(2)}, u32[]{:S(2)}) collective-permute-start(bf16[768,256]{1,0:T(8,128)(2,1)S(1)} %copy-done.1), channel_id=1, source_target_pairs={{0,496},{16,0},{32,16},{48,32},{64,48},{80,64},{96,80},{112,96},{1... | collective-permute-start | bytes 1179656 | tf_op jit(solution)/shard_map/ppermute | solution.py:255
  120.6 14.5 %collective-permute-start.8 = (bf16[512,256]{1,0:T(8,128)(2,1)S(1)}, bf16[512,256]{1,0:T(8,128)(2,1)S(1)}, u32[]{:S(2)}, u32[]{:S(2)}) collective-permute-start(bf16[512,256]{1,0:T(8,128)(2,1)S(1)} %copy-done.6), channel_id=1, source_target_pairs={{0,32},{8,232},{16,48},{24,248},{32,64},{40,8},{48,80},{56,24},{64... | collective-permute-start | bytes 786440 | tf_op jit(solution)/shard_map/ppermute | solution.py:278
  137.4 4.2 %collective-permute-start.9 = (bf16[256,128]{1,0:T(8,128)(2,1)S(1)}, bf16[256,128]{1,0:T(8,128)(2,1)S(1)}, u32[]{:S(2)}, u32[]{:S(2)}) collective-permute-start(bf16[256,128]{1,0:T(8,128)(2,1)S(1)} %shard_map.74), channel_id=1, source_target_pairs={{0,8},{8,0},{1,9},{9,1},{2,10},{10,2},{3,11},{11,3},{4,12},{12,4},... | collective-permute-start | bytes 196616 | tf_op jit(solution)/shard_map/ppermute | solution.py:242
Sparse Core Ops, SparseCore 0:
  25.2 67.6 all-gather.1

commit v2 on v1

--- a/solution.py
+++ b/solution.py
@@ -45,6 +45,7 @@
     return pl.pallas_call(
         pack_kernel,
         out_shape=jax.ShapeDtypeStruct((copies * heads, w.shape[1], 4 * HEAD), BF16),
+        compiler_params=pltpu.CompilerParams(vmem_limit_bytes=4 << 20),
         name="pack",
     )(w, o)
 
@@ -177,16 +178,16 @@
     def _():
         near[pl.ds(2 * count, count)] = after_ref[lines]
 
-    scale = 1.0 / math.sqrt(HEAD)
+    scale = math.log2(math.e) / math.sqrt(HEAD)
     q = q_ref[slab]
     lines = pl.ds(0, style)
     refs = [near, *(r.at[lines] for r in (forward_ref, before_ref, after_ref)), far_ref]
     scores = []
     for n, ref in enumerate(refs):
-        part = lax.dot_general(q, ref[:, :HEAD], NT, preferred_element_type=F32) * scale
+        part = lax.dot_general(q, ref[:, :HEAD], NT, preferred_element_type=F32)
         scores.append(jnp.where(flag_ref[0, 0] > 0, part, -1e30) if n else part)
     peak = functools.reduce(jnp.maximum, [jnp.max(s, axis=-1, keepdims=True) for s in scores])
-    expo = [jnp.exp(s - peak) for s in scores]
+    expo = [jnp.exp2((s - peak) * scale) for s in scores]
     share = 1.0 / sum(jnp.sum(e, axis=-1, keepdims=True) for e in expo)
     o_ref[...] = sum(
         jnp.dot((e * share).astype(BF16), ref[:, HEAD:], preferred_element_type=F32)

time: 177 us -> 176 us (level)
  no operation moved by 1% of the time
where the time goes in v2:
time: 176 us; the launch traced here: 175 us
  starting transfers between devices  66.2 us (38%)
  blocking collectives  41.3 us (23%)
  waiting for transfers between devices  33.6 us (19%)
  between operations  14.3 us (8%)
  Pallas kernels  11.7 us (7%)
  local copies, waits for them, and re-layouts  6.65 us (4%)
    ppermute x5, starting transfers between devices, shift(): lax.ppermute(block, axes, [(i, (i + by) % count) for i in range(count)])  29.9 us
    ppermute x5, starting transfers between devices, swap(): return lax.ppermute(block, 'core', [(0, 1), (1, 0)])  25.6 us
    all_to_all x1, blocking collectives, local(): shares = lax.all_to_all(shares, TP, 0, 0, tiled=True)  25.3 us
    all_to_all x1, blocking collectives, local(): plane = lax.all_to_all(mine, ('x_hi', 'core'), 0, 0, tiled=True)  16 us
    all_to_all x2, waiting for transfers between devices, spread(): lax.all_to_all(jnp.broadcast_to(block[None], (count,) + block.shape), axe...  14.5 us
    ppermute x1, waiting for transfers between devices, local(): far = lax.ppermute(far, Z + ('core',), pairs)  12.6 us
    all_to_all x2, starting transfers between devices, spread(): lax.all_to_all(jnp.broadcast_to(block[None], (count,) + block.shape), axe...  8.75 us
    pallas_call x1, Pallas kernels, project(): pl.pallas_call(project_kernel, in_specs=[pl.BlockSpec(memory_space=pltpu....  7.13 us
  transfers between devices with their start and end apart: 14, of which 5 were waited for; matrix products, arithmetic and copies ran while one was open for 2% of the time, Pallas kernels for 2%

profile of v2, /device:TPU:1, one launch (start us, length us, event | category | flops | bytes accessed | tf_op | source)
XLA Modules:
  0.0 174.7 jit_solution(16285996262929129769)
XLA Ops:
  6.5 0.0 all-gather.2.cloned.1.call-start
  6.5 0.9 copy-done.3
  7.4 0.7 copy-done.4
  8.2 16.0 %all_to_all.20 = bf16[4,48,512]{2,1,0:T(8,128)(2,1)} all-to-all(bf16[4,48,512]{2,1,0:T(8,128)(2,1)S(1)} %pack.1), channel_id=1, replica_groups=mesh['x_hi'=2,'z_hi'=4,'z_lo'=4,'core'=2,'y'=4,'x_lo'=2] {'x_hi','core'}, dimensions={0} | all-to-all | bytes 393216 | tf_op jit(solution)/shard_map/all_to_all | solution.py:247
  24.1 0.0 all-gather.2.cloned.1.call-update
  24.2 2.2 %broadcast_in_dim.4 = bf16[8,256,384]{2,1,0:T(8,128)(2,1)} broadcast(bf16[256,384]{1,0:T(8,128)(2,1)} %param.7), dimensions={1,2} | broadcast | bytes 1769472 | tf_op jit(solution)/shard_map/broadcast_in_dim | solution.py:24
  26.4 3.7 %all-to-all-start.1 = ((bf16[8,256,384]{2,1,0:T(8,128)(2,1)}), bf16[8,256,384]{2,1,0:T(8,128)(2,1)S(1)}, u32[]{:S(2)}, u32[]{:S(2)}) async-start(bf16[8,256,384]{2,1,0:T(8,128)(2,1)} %broadcast_in_dim.4), calls=%async_computation.1 | async-start | bytes 3145728 | tf_op jit(solution)/shard_map/all_to_all | solution.py:23
  30.1 0.0 copy-done.7
  30.1 5.2 %collective-permute-start.1 = (bf16[32,384]{1,0:T(8,128)(2,1)S(1)}, bf16[32,384]{1,0:T(8,128)(2,1)S(1)}, u32[]{:S(2)}, u32[]{:S(2)}) collective-permute-start(bf16[32,384]{1,0:T(8,128)(2,1)S(1)} %copy-done.7), channel_id=1, source_target_pairs={{0,64},{16,80},{32,96},{48,112},{64,128},{80,144},{96,160},{112,17... | collective-permute-start | bytes 73736 | tf_op jit(solution)/shard_map/ppermute | solution.py:256
  35.4 10.6 %collective-permute-start.2 = (bf16[32,384]{1,0:T(8,128)(2,1)S(1)}, bf16[32,384]{1,0:T(8,128)(2,1)S(1)}, u32[]{:S(2)}, u32[]{:S(2)}) collective-permute-start(bf16[32,384]{1,0:T(8,128)(2,1)S(1)} %copy-done.7), channel_id=1, source_target_pairs={{0,128},{16,144},{32,160},{48,176},{64,192},{80,208},{96,224},{112... | collective-permute-start | bytes 73736 | tf_op jit(solution)/shard_map/ppermute | solution.py:256
  46.0 5.2 %collective-permute-start.3 = (bf16[32,384]{1,0:T(8,128)(2,1)S(1)}, bf16[32,384]{1,0:T(8,128)(2,1)S(1)}, u32[]{:S(2)}, u32[]{:S(2)}) collective-permute-start(bf16[32,384]{1,0:T(8,128)(2,1)S(1)} %copy-done.7), channel_id=1, source_target_pairs={{0,192},{16,208},{32,224},{48,240},{64,0},{80,16},{96,32},{112,48}... | collective-permute-start | bytes 73736 | tf_op jit(solution)/shard_map/ppermute | solution.py:256
  51.2 0.0 collective-permute-done.1
  51.2 0.0 collective-permute-done.2
  51.2 4.3 %collective-permute-done.3 = bf16[32,384]{1,0:T(8,128)(2,1)S(1)} collective-permute-done((bf16[32,384]{1,0:T(8,128)(2,1)S(1)}, bf16[32,384]{1,0:T(8,128)(2,1)S(1)}, u32[]{:S(2)}, u32[]{:S(2)}) %collective-permute-start.3) | collective-permute-done | bytes 24608 | tf_op jit(solution)/shard_map/ppermute | solution.py:256
  55.5 0.0 all-to-all-done.1.x_ref
  55.5 0.0 copy-start.5
  55.5 1.5 broadcast_in_dim.5
  57.0 5.0 %all-to-all-start.2 = ((bf16[16,128,384]{2,1,0:T(8,128)(2,1)}), bf16[16,128,384]{2,1,0:T(8,128)(2,1)S(1)}, u32[]{:S(2)}, u32[]{:S(2)}) async-start(bf16[16,128,384]{2,1,0:T(8,128)(2,1)} %broadcast_in_dim.5), calls=%async_computation.2 | async-start | bytes 3145728 | tf_op jit(solution)/shard_map/all_to_all | solution.py:23
  62.1 0.0 copy-done.5
  62.1 5.1 %collective-permute-start = (bf16[8,256,384]{2,1,0:T(8,128)(2,1)S(1)}, bf16[8,256,384]{2,1,0:T(8,128)(2,1)}, u32[]{:S(2)}, u32[]{:S(2)}) collective-permute-start(bf16[8,256,384]{2,1,0:T(8,128)(2,1)S(1)} %all-to-all-done.1.x_ref), channel_id=1, source_target_pairs={{0,8},{8,0},{1,9},{9,1},{2,10},{10,2},{3,11},{11,3},{4,12},{12,4},... | collective-permute-start | bytes 4718600 | tf_op jit(solution)/shard_map/ppermute | solution.py:243
  67.2 14.5 %all-to-all-done.2 = bf16[16,128,384]{2,1,0:T(8,128)(2,1)S(1)} async-done(((bf16[16,128,384]{2,1,0:T(8,128)(2,1)}), bf16[16,128,384]{2,1,0:T(8,128)(2,1)S(1)}, u32[]{:S(2)}, u32[]{:S(2)}) %all-to-all-start.2) | async-done | bytes 1572896 | tf_op jit(solution)/shard_map/all_to_all | solution.py:23
  81.7 6.2 %collective-permute-start.4 = (bf16[2,8,128,384]{3,2,1,0:T(8,128)(2,1)S(1)}, bf16[2,8,128,384]{3,2,1,0:T(8,128)(2,1)}, u32[]{:S(2)}, u32[]{:S(2)}) collective-permute-start(bf16[2,8,128,384]{3,2,1,0:T(8,128)(2,1)S(1)} %bitcast.8), channel_id=1, source_target_pairs={{0,8},{8,0},{1,9},{9,1},{2,10},{10,2},{3,11},{11,3},{4,12},{12,4},... | collective-permute-start | bytes 4718600 | tf_op jit(solution)/shard_map/ppermute | solution.py:243
  88.0 1.9 %collective-permute-start.5 = (s32[1,1]{1,0:T(1,128)}, s32[1,1]{1,0:T(1,128)}, u32[]{:S(2)}, u32[]{:S(2)}) collective-permute-start(s32[1,1]{1,0:T(1,128)} %param.13), channel_id=1, source_target_pairs={{0,8},{8,0},{1,9},{9,1},{2,10},{10,2},{3,11},{11,3},{4,12},{12,4},... | collective-permute-start | bytes 20 | tf_op jit(solution)/shard_map/ppermute | solution.py:243
  89.9 1.2 collective-permute-done.5.flag_ref
  91.1 0.0 collective-permute-done.y_ref
  91.1 0.0 collective-permute-done.4.sy_ref
  91.1 1.0 all-gather.2.cloned.1.call-done
  92.1 0.0 copy-done.6
  92.1 7.1 %project.1 = (bf16[768,256]{1,0:T(8,128)(2,1)}, bf16[768,256]{1,0:T(8,128)(2,1)}, bf16[512,256]{1,0:T(8,128)(2,1)}, bf16[2,256,128]{2,1,0:T(8,128)(2,1)}) custom-call(s32[1]{0:T(128)} %bitcast.me_ref, bf16[8,256,384]{2,1,0:T(8,128)(2,1)} %copy-done.5, bf16[8,256,384]{2,1,0:T(8,128)(2,1)} %collective-permute-done.y_ref, bf16[2,8,128,384]{3,2,1,0:T(8,128)(2,1)} %bitcast.9, ...), custom_call_target="tpu_custom_call" | custom-call | tf_op jit(solution)/shard_map/project/pallas_call | solution.py:133
  99.3 0.0 copy-start.2
  99.3 1.3 slice.3.wx_ref
  100.6 10.4 %collective-permute-start.10 = (bf16[3072,128]{1,0:T(8,128)(2,1)S(1)}, bf16[3072,128]{1,0:T(8,128)(2,1)S(1)}, u32[]{:S(2)}, u32[]{:S(2)}) collective-permute-start(bf16[3072,128]{1,0:T(8,128)(2,1)S(1)} %slice.3.wx_ref), channel_id=1, source_target_pairs={{0,8},{8,0},{1,9},{9,1},{2,10},{10,2},{3,11},{11,3},{4,12},{12,4},... | collective-permute-start | bytes 2359304 | tf_op jit(solution)/shard_map/ppermute | solution.py:243
  111.0 2.6 %collective-permute-start.6 = (bf16[768,256]{1,0:T(8,128)(2,1)S(1)}, bf16[768,256]{1,0:T(8,128)(2,1)S(1)}, u32[]{:S(2)}, u32[]{:S(2)}) collective-permute-start(bf16[768,256]{1,0:T(8,128)(2,1)S(1)} %copy-done), channel_id=1, source_target_pairs={{0,16},{16,32},{32,48},{48,64},{64,80},{80,96},{96,112},{112,128},... | collective-permute-start | bytes 1179656 | tf_op jit(solution)/shard_map/ppermute | solution.py:256
  113.6 0.0 copy-done.1
  113.6 6.3 %collective-permute-start.7 = (bf16[768,256]{1,0:T(8,128)(2,1)S(1)}, bf16[768,256]{1,0:T(8,128)(2,1)S(1)}, u32[]{:S(2)}, u32[]{:S(2)}) collective-permute-start(bf16[768,256]{1,0:T(8,128)(2,1)S(1)} %copy-done.1), channel_id=1, source_target_pairs={{0,496},{16,0},{32,16},{48,32},{64,48},{80,64},{96,80},{112,96},{1... | collective-permute-start | bytes 1179656 | tf_op jit(solution)/shard_map/ppermute | solution.py:256
  119.9 1.9 %collective-permute-start.8 = (bf16[512,256]{1,0:T(8,128)(2,1)S(1)}, bf16[512,256]{1,0:T(8,128)(2,1)S(1)}, u32[]{:S(2)}, u32[]{:S(2)}) collective-permute-start(bf16[512,256]{1,0:T(8,128)(2,1)S(1)} %copy-done.8), channel_id=1, source_target_pairs={{0,32},{8,232},{16,48},{24,248},{32,64},{40,8},{48,80},{56,24},{64... | collective-permute-start | bytes 786440 | tf_op jit(solution)/shard_map/ppermute | solution.py:279
  121.9 12.6 %collective-permute-done.8.far_ref = bf16[512,256]{1,0:T(8,128)(2,1)S(1)} collective-permute-done((bf16[512,256]{1,0:T(8,128)(2,1)S(1)}, bf16[512,256]{1,0:T(8,128)(2,1)S(1)}, u32[]{:S(2)}, u32[]{:S(2)}) %collective-permute-start.8) | collective-permute-done | bytes 262176 | tf_op jit(solution)/shard_map/ppermute | solution.py:279
  134.5 0.0 collective-permute-done.6.before_ref
  134.5 0.0 collective-permute-done.7.after_ref
  134.5 0.0 copy-done.2
  134.5 2.3 %shard_map.74 = bf16[256,128]{1,0:T(8,128)(2,1)S(1)} custom-call(s32[1]{0:T(128)} %bitcast.me_ref, s32[1,1]{1,0:T(1,128)} %collective-permute-done.5.flag_ref, bf16[2,256,128]{2,1,0:T(8,128)(2,1)S(1)} %copy-done.2, bf16[768,256]{1,0:T(8,128)(2,1)S(1)} %copy-done, bf16[768,256]{1,0:T(8,128)(2,1)S(1)} %copy-done.1, ...), custom_call_target="tpu_custom_call" | custom-call | flops 369098752 | bytes 2097152 | tf_op jit(solution)/shard_map/pallas_call | solution.py:202
  136.7 1.9 %collective-permute-start.9 = (bf16[256,128]{1,0:T(8,128)(2,1)S(1)}, bf16[256,128]{1,0:T(8,128)(2,1)S(1)}, u32[]{:S(2)}, u32[]{:S(2)}) collective-permute-start(bf16[256,128]{1,0:T(8,128)(2,1)S(1)} %shard_map.74), channel_id=1, source_target_pairs={{0,8},{8,0},{1,9},{9,1},{2,10},{10,2},{3,11},{11,3},{4,12},{12,4},... | collective-permute-start | bytes 196616 | tf_op jit(solution)/shard_map/ppermute | solution.py:243
  139.3 1.6 shard_map.73.ax_ref
  140.9 0.0 collective-permute-done.9.ay_ref
  140.9 0.0 collective-permute-done.10.wy_ref
  140.9 0.7 mix.1
  141.7 25.3 %all_to_all.21 = bf16[8,256,384]{2,1,0:T(8,128)(2,1)S(1)} all-to-all(bf16[8,256,384]{2,1,0:T(8,128)(2,1)S(1)} %mix.1), channel_id=1, replica_groups=mesh['x_hi'=2,'z_hi'=4,'z_lo'=4,'core'=2,'y'=4,'x_lo'=2] {'y','x_lo'}, dimensions={0} | all-to-all | bytes 3145728 | tf_op jit(solution)/shard_map/all_to_all | solution.py:288
  166.9 0.9 reduce_sum.12
  (11 shorter events, 0.0 us)
Async XLA Ops:
  6.5 85.6 %all-gather.2.cloned.1.call-start = ((), (), s32[]{:S(2)}) async-start(), calls=%async_computation.4 | async-start | bytes 3342336 | tf_op jit(solution)/shard_map/all_gather | solution.py:249
  6.5 0.9 copy-start.3
  7.4 0.7 copy-start.4
  26.4 3.7 %copy-start.7 = (bf16[32,384]{1,0:T(8,128)(2,1)S(1)}, bf16[32,384]{1,0:T(8,128)(2,1)}, u32[]{:S(2)}) copy-start(bf16[32,384]{1,0:T(8,128)(2,1)} %param.8) | copy-start | bytes 73732
  26.4 29.1 %all-to-all-start.1 = ((bf16[8,256,384]{2,1,0:T(8,128)(2,1)}), bf16[8,256,384]{2,1,0:T(8,128)(2,1)S(1)}, u32[]{:S(2)}, u32[]{:S(2)}) async-start(bf16[8,256,384]{2,1,0:T(8,128)(2,1)} %broadcast_in_dim.4), calls=%async_computation.1 | async-start | bytes 3145728 | tf_op jit(solution)/shard_map/all_to_all | solution.py:23
  30.1 21.1 %collective-permute-start.1 = (bf16[32,384]{1,0:T(8,128)(2,1)S(1)}, bf16[32,384]{1,0:T(8,128)(2,1)S(1)}, u32[]{:S(2)}, u32[]{:S(2)}) collective-permute-start(bf16[32,384]{1,0:T(8,128)(2,1)S(1)} %copy-done.7), channel_id=1, source_target_pairs={{0,64},{16,80},{32,96},{48,112},{64,128},{80,144},{96,160},{112,17... | collective-permute-start | bytes 73736 | tf_op jit(solution)/shard_map/ppermute | solution.py:256
  35.4 15.8 %collective-permute-start.2 = (bf16[32,384]{1,0:T(8,128)(2,1)S(1)}, bf16[32,384]{1,0:T(8,128)(2,1)S(1)}, u32[]{:S(2)}, u32[]{:S(2)}) collective-permute-start(bf16[32,384]{1,0:T(8,128)(2,1)S(1)} %copy-done.7), channel_id=1, source_target_pairs={{0,128},{16,144},{32,160},{48,176},{64,192},{80,208},{96,224},{112... | collective-permute-start | bytes 73736 | tf_op jit(solution)/shard_map/ppermute | solution.py:256
  46.0 9.5 %collective-permute-start.3 = (bf16[32,384]{1,0:T(8,128)(2,1)S(1)}, bf16[32,384]{1,0:T(8,128)(2,1)S(1)}, u32[]{:S(2)}, u32[]{:S(2)}) collective-permute-start(bf16[32,384]{1,0:T(8,128)(2,1)S(1)} %copy-done.7), channel_id=1, source_target_pairs={{0,192},{16,208},{32,224},{48,240},{64,0},{80,16},{96,32},{112,48}... | collective-permute-start | bytes 73736 | tf_op jit(solution)/shard_map/ppermute | solution.py:256
  55.5 6.6 %copy-start.5 = (bf16[8,256,384]{2,1,0:T(8,128)(2,1)}, bf16[8,256,384]{2,1,0:T(8,128)(2,1)S(1)}, u32[]{:S(2)}) copy-start(bf16[8,256,384]{2,1,0:T(8,128)(2,1)S(1)} %all-to-all-done.1.x_ref) | copy-start | bytes 4718596
  57.0 24.7 %all-to-all-start.2 = ((bf16[16,128,384]{2,1,0:T(8,128)(2,1)}), bf16[16,128,384]{2,1,0:T(8,128)(2,1)S(1)}, u32[]{:S(2)}, u32[]{:S(2)}) async-start(bf16[16,128,384]{2,1,0:T(8,128)(2,1)} %broadcast_in_dim.5), calls=%async_computation.2 | async-start | bytes 3145728 | tf_op jit(solution)/shard_map/all_to_all | solution.py:23
  62.1 29.0 %collective-permute-start = (bf16[8,256,384]{2,1,0:T(8,128)(2,1)S(1)}, bf16[8,256,384]{2,1,0:T(8,128)(2,1)}, u32[]{:S(2)}, u32[]{:S(2)}) collective-permute-start(bf16[8,256,384]{2,1,0:T(8,128)(2,1)S(1)} %all-to-all-done.1.x_ref), channel_id=1, source_target_pairs={{0,8},{8,0},{1,9},{9,1},{2,10},{10,2},{3,11},{11,3},{4,12},{12,4},... | collective-permute-start | bytes 4718600 | tf_op jit(solution)/shard_map/ppermute | solution.py:243
  81.7 10.4 %copy-start.6 = (bf16[16,128,384]{2,1,0:T(8,128)(2,1)}, bf16[16,128,384]{2,1,0:T(8,128)(2,1)S(1)}, u32[]{:S(2)}) copy-start(bf16[16,128,384]{2,1,0:T(8,128)(2,1)S(1)} %all-to-all-done.2) | copy-start | bytes 4718596
  81.7 9.4 %collective-permute-start.4 = (bf16[2,8,128,384]{3,2,1,0:T(8,128)(2,1)S(1)}, bf16[2,8,128,384]{3,2,1,0:T(8,128)(2,1)}, u32[]{:S(2)}, u32[]{:S(2)}) collective-permute-start(bf16[2,8,128,384]{3,2,1,0:T(8,128)(2,1)S(1)} %bitcast.8), channel_id=1, source_target_pairs={{0,8},{8,0},{1,9},{9,1},{2,10},{10,2},{3,11},{11,3},{4,12},{12,4},... | collective-permute-start | bytes 4718600 | tf_op jit(solution)/shard_map/ppermute | solution.py:243
  88.0 3.2 %collective-permute-start.5 = (s32[1,1]{1,0:T(1,128)}, s32[1,1]{1,0:T(1,128)}, u32[]{:S(2)}, u32[]{:S(2)}) collective-permute-start(s32[1,1]{1,0:T(1,128)} %param.13), channel_id=1, source_target_pairs={{0,8},{8,0},{1,9},{9,1},{2,10},{10,2},{3,11},{11,3},{4,12},{12,4},... | collective-permute-start | bytes 20 | tf_op jit(solution)/shard_map/ppermute | solution.py:243
  99.3 11.7 %copy-start = (bf16[768,256]{1,0:T(8,128)(2,1)S(1)}, bf16[768,256]{1,0:T(8,128)(2,1)}, u32[]{:S(2)}) copy-start(bf16[768,256]{1,0:T(8,128)(2,1)} %get-tuple-element.30.forward_ref) | copy-start | bytes 1179652
  99.3 14.3 %copy-start.1 = (bf16[768,256]{1,0:T(8,128)(2,1)S(1)}, bf16[768,256]{1,0:T(8,128)(2,1)}, u32[]{:S(2)}) copy-start(bf16[768,256]{1,0:T(8,128)(2,1)} %get-tuple-element.31.backward_ref) | copy-start | bytes 1179652
  99.3 20.6 %copy-start.8 = (bf16[512,256]{1,0:T(8,128)(2,1)S(1)}, bf16[512,256]{1,0:T(8,128)(2,1)}, u32[]{:S(2)}) copy-start(bf16[512,256]{1,0:T(8,128)(2,1)} %get-tuple-element.32) | copy-start | bytes 786436
  99.3 35.2 %copy-start.2 = (bf16[2,256,128]{2,1,0:T(8,128)(2,1)S(1)}, bf16[2,256,128]{2,1,0:T(8,128)(2,1)}, u32[]{:S(2)}) copy-start(bf16[2,256,128]{2,1,0:T(8,128)(2,1)} %get-tuple-element.29.q_ref) | copy-start | bytes 393220
  100.6 40.3 %collective-permute-start.10 = (bf16[3072,128]{1,0:T(8,128)(2,1)S(1)}, bf16[3072,128]{1,0:T(8,128)(2,1)S(1)}, u32[]{:S(2)}, u32[]{:S(2)}) collective-permute-start(bf16[3072,128]{1,0:T(8,128)(2,1)S(1)} %slice.3.wx_ref), channel_id=1, source_target_pairs={{0,8},{8,0},{1,9},{9,1},{2,10},{10,2},{3,11},{11,3},{4,12},{12,4},... | collective-permute-start | bytes 2359304 | tf_op jit(solution)/shard_map/ppermute | solution.py:243
  111.0 23.5 %collective-permute-start.6 = (bf16[768,256]{1,0:T(8,128)(2,1)S(1)}, bf16[768,256]{1,0:T(8,128)(2,1)S(1)}, u32[]{:S(2)}, u32[]{:S(2)}) collective-permute-start(bf16[768,256]{1,0:T(8,128)(2,1)S(1)} %copy-done), channel_id=1, source_target_pairs={{0,16},{16,32},{32,48},{48,64},{64,80},{80,96},{96,112},{112,128},... | collective-permute-start | bytes 1179656 | tf_op jit(solution)/shard_map/ppermute | solution.py:256
  113.6 20.9 %collective-permute-start.7 = (bf16[768,256]{1,0:T(8,128)(2,1)S(1)}, bf16[768,256]{1,0:T(8,128)(2,1)S(1)}, u32[]{:S(2)}, u32[]{:S(2)}) collective-permute-start(bf16[768,256]{1,0:T(8,128)(2,1)S(1)} %copy-done.1), channel_id=1, source_target_pairs={{0,496},{16,0},{32,16},{48,32},{64,48},{80,64},{96,80},{112,96},{1... | collective-permute-start | bytes 1179656 | tf_op jit(solution)/shard_map/ppermute | solution.py:256
  119.9 14.5 %collective-permute-start.8 = (bf16[512,256]{1,0:T(8,128)(2,1)S(1)}, bf16[512,256]{1,0:T(8,128)(2,1)S(1)}, u32[]{:S(2)}, u32[]{:S(2)}) collective-permute-start(bf16[512,256]{1,0:T(8,128)(2,1)S(1)} %copy-done.8), channel_id=1, source_target_pairs={{0,32},{8,232},{16,48},{24,248},{32,64},{40,8},{48,80},{56,24},{64... | collective-permute-start | bytes 786440 | tf_op jit(solution)/shard_map/ppermute | solution.py:279
  136.7 4.2 %collective-permute-start.9 = (bf16[256,128]{1,0:T(8,128)(2,1)S(1)}, bf16[256,128]{1,0:T(8,128)(2,1)S(1)}, u32[]{:S(2)}, u32[]{:S(2)}) collective-permute-start(bf16[256,128]{1,0:T(8,128)(2,1)S(1)} %shard_map.74), channel_id=1, source_target_pairs={{0,8},{8,0},{1,9},{9,1},{2,10},{10,2},{3,11},{11,3},{4,12},{12,4},... | collective-permute-start | bytes 196616 | tf_op jit(solution)/shard_map/ppermute | solution.py:243
Sparse Core Ops, SparseCore 0:
  24.3 67.8 all-gather.1
